TPU v7x, 256 devices: a whole 4x4x8 slice. The times are simulated.
256 devices in a mesh: segment: 8 (over x_lo, y), lat: 16 (over z, x_hi), dp: 2 (over core).
Axes of the slice: x: 4 (x_hi: 2, x_lo: 2; x = x_hi * 2 + x_lo), y: 4, z: 8, core: 2. Of those that a mesh axis runs over, the one named last changes fastest.
Arguments:
- initial: bfloat16 [8, 192, 32, 128], P('dp', None, 'lat'), may hold values from -6 to 6
- kernel: bfloat16 [8, 192, 9, 192], P('segment'), may hold values from -0.078125 to 0.078125
- bias: float32 [8, 192], P('segment'), may hold values from -0.6 to 0.6
- cotangent: bfloat16 [2, 8, 192, 32, 128], P(None, 'dp', None, 'lat'), may hold values from -6 to 6
Outputs:
- section_out: bfloat16 [8, 8, 192, 32, 128], P('segment', 'dp', None, 'lat')
- state_adjoint: float32 [8, 8, 192, 32, 128], P('segment', 'dp', None, 'lat')
- kernel_grad: float32 [8, 192, 9, 192], P('segment')
- bias_grad: float32 [8, 192], P('segment')
All inputs are finite; a program needn't handle non-finite values.
Results may differ from a plain program's by a relative error of at most 0.028.
Values may be sent and summed in bfloat16 or wider, within the bound.
A program may use at most 64 MiB of HBM per device.

v0:
```python
import math
import jax
import jax.numpy as jnp
from jax import lax
from jax.sharding import PartitionSpec as P

STEPS = 2


def passed_along(value, axis, steps):
    count = lax.axis_size(axis)
    pairs = [(source, (source + steps) % count) for source in range(count)]
    return lax.ppermute(value, axis, pairs)


def padded_2(block, sides, width):
    for axis, dim in sides:
        count = lax.axis_size(axis)
        forward = [(i, i + 1) for i in range(count - 1)]
        backward = [(target, source) for source, target in forward]
        low = lax.ppermute(
            lax.slice_in_dim(block, block.shape[dim] - width, None, axis=dim), axis, forward
        )
        high = lax.ppermute(lax.slice_in_dim(block, 0, width, axis=dim), axis, backward)
        block = jnp.concatenate([low, block, high], axis=dim)
    return block


def silu_value(values):
    return values / (1.0 + jnp.exp(-values))


def silu_slope(values):
    sigmoid_v = 1.0 / (1.0 + jnp.exp(-values))
    return sigmoid_v * (1.0 + values * (1.0 - sigmoid_v))


def tap_columns(padded):
    band_rows = padded.shape[1] - 2
    pieces = []
    for row_tap in range(3):
        strip = padded[:, row_tap : row_tap + band_rows, :]
        for col_tap in range(3):
            pieces.append(jnp.roll(strip, 1 - col_tap, axis=2))
    stacked = jnp.stack(pieces, axis=0)
    return stacked.reshape(9 * padded.shape[0], band_rows * padded.shape[2])


def back_columns(padded):
    band_rows = padded.shape[1] - 2
    pieces = []
    for row_tap in range(3):
        strip = padded[:, 2 - row_tap : 2 - row_tap + band_rows, :]
        for col_tap in range(3):
            pieces.append(jnp.roll(strip, col_tap - 1, axis=2))
    stacked = jnp.stack(pieces, axis=0)
    return stacked.reshape(9, padded.shape[0], band_rows * padded.shape[2])


def take_slot(buffer, slot):
    return lax.dynamic_index_in_dim(buffer, slot, 0, keepdims=False)


def put_slot(buffer, slot, value, flag):
    previous = lax.dynamic_index_in_dim(buffer, slot, 0, keepdims=False)
    return lax.dynamic_update_index_in_dim(buffer, jnp.where(flag, value, previous), slot, 0)


def per_device(initial, kernel, bias, cotangent):
    segment_count = lax.axis_size("segment")
    position = lax.axis_index("segment")
    before = jnp.mod(position - 1, segment_count)
    after = jnp.mod(position + 1, segment_count)
    micro = initial.shape[0]
    channels = initial.shape[1]
    band_rows = initial.shape[2]
    longitude = initial.shape[3]
    band_shape = (channels, band_rows, longitude)
    applications = STEPS * segment_count
    flat_kernel = kernel[0].reshape(channels, 9 * channels)
    kernel_taps = kernel[0]
    offsets = bias[0][:, None, None]
    cot_flat = cotangent.reshape((STEPS * micro,) + band_shape)
    tick_count = STEPS * (segment_count + micro - 1)

    def plan(moment, where_at):
        phase_span = segment_count + micro - 1
        rollout_step = jnp.floor_divide(moment, phase_span)
        sample = moment - rollout_step * phase_span - where_at
        applied = rollout_step * segment_count + where_at
        active = (moment >= 0) & (rollout_step < STEPS) & (sample >= 0) & (sample < micro)
        return (jnp.clip(sample, 0, micro - 1), applied, active)

    zero_band = jnp.zeros(band_shape, jnp.bfloat16)
    acts_store = jnp.zeros((STEPS * micro, channels, band_rows + 2, longitude), jnp.bfloat16)

    def forward_tick(moment, carry):
        outgoing, arrived, saved_states, acts_kept, last_outputs = carry
        received = passed_along(outgoing, "segment", 1)
        sent_sample, sent_applied, sent_active = plan(moment - 1, before)
        arrived = put_slot(
            arrived, sent_sample, received, sent_active & (sent_applied < applications - 1)
        )
        sample, applied, active = plan(moment, position)
        current = jnp.where(applied == 0, take_slot(initial, sample), take_slot(arrived, sample))
        activated = silu_value(current.astype(jnp.float32)).astype(jnp.bfloat16)
        padded = padded_2(activated, (("lat", 1),), 1)

        def advance(unused):
            branch = jnp.dot(
                flat_kernel, tap_columns(padded), preferred_element_type=jnp.float32
            ).reshape(band_shape)
            return (current.astype(jnp.float32) + branch + offsets).astype(jnp.bfloat16)

        def holding(unused):
            return current

        produced = lax.cond(active, advance, holding, 0)
        slot = jnp.clip(applied // segment_count, 0, STEPS - 1) * micro + sample
        saved_states = put_slot(saved_states, slot, current, active)
        acts_kept = put_slot(acts_kept, slot, padded, active)
        last_outputs = put_slot(
            last_outputs, sample, produced, active & (applied >= applications - segment_count)
        )
        return (produced, arrived, saved_states, acts_kept, last_outputs)

    forward_start = (
        zero_band,
        jnp.zeros((micro,) + band_shape, jnp.bfloat16),
        jnp.zeros((STEPS * micro,) + band_shape, jnp.bfloat16),
        acts_store,
        jnp.zeros((micro,) + band_shape, jnp.bfloat16),
    )
    unused_out, unused_arrived, saved_states, acts_kept, last_outputs = lax.fori_loop(
        0, tick_count, forward_tick, forward_start
    )

    def backward_tick(turn, carry):
        outgoing, arrived, adjoints, kernel_sum, bias_sum = carry
        received = passed_along(outgoing, "segment", -1)
        sent_sample, sent_applied, sent_active = plan(tick_count - turn, after)
        arrived = put_slot(arrived, sent_sample, received, sent_active & (sent_applied >= 1))
        sample, applied, active = plan(tick_count - 1 - turn, position)
        incoming = jnp.where(
            applied == applications - 1,
            take_slot(cot_flat, (STEPS - 1) * micro + sample),
            take_slot(arrived, sample),
        )
        incoming_padded = padded_2(incoming, (("lat", 1),), 1)
        slot = jnp.clip(applied // segment_count, 0, STEPS - 1) * micro + sample
        current = take_slot(saved_states, slot)
        padded = take_slot(acts_kept, slot)
        step_end = (applied >= segment_count) & (jnp.mod(applied, segment_count) == 0)
        cot_slot = jnp.clip(applied // segment_count - 1, 0, STEPS - 1) * micro + sample

        def retreat(unused):
            gradient_rows = incoming.reshape(channels, band_rows * longitude)
            kernel_term = lax.dot_general(
                gradient_rows,
                tap_columns(padded),
                (((1,), (1,)), ((), ())),
                preferred_element_type=jnp.float32,
            )
            bias_term = jnp.sum(incoming.astype(jnp.float32), axis=(1, 2))
            transposed = lax.dot_general(
                kernel_taps,
                back_columns(incoming_padded),
                (((0, 1), (1, 0)), ((), ())),
                preferred_element_type=jnp.float32,
            ).reshape(band_shape)
            adjoint_here = (
                incoming.astype(jnp.float32) + silu_slope(current.astype(jnp.float32)) * transposed
            )
            adjoint_here = adjoint_here + jnp.where(
                step_end, take_slot(cot_flat, cot_slot).astype(jnp.float32), 0.0
            )
            return (kernel_sum + kernel_term, bias_sum + bias_term, adjoint_here)

        def resting(unused):
            return (kernel_sum, bias_sum, jnp.zeros(band_shape, jnp.float32))

        kernel_sum, bias_sum, adjoint_here = lax.cond(active, retreat, resting, 0)
        adjoints = put_slot(adjoints, sample, adjoint_here, active & (applied < segment_count))
        return (adjoint_here.astype(jnp.bfloat16), arrived, adjoints, kernel_sum, bias_sum)

    backward_start = (
        zero_band,
        jnp.zeros((micro,) + band_shape, jnp.bfloat16),
        jnp.zeros((micro,) + band_shape, jnp.float32),
        jnp.zeros((channels, 9 * channels), jnp.float32),
        jnp.zeros((channels,), jnp.float32),
    )
    unused_grad, unused_inbox, adjoints, kernel_sum, bias_sum = lax.fori_loop(
        0, tick_count, backward_tick, backward_start
    )
    kernel_total, bias_total = (
        lax.psum(kernel_sum.astype(jnp.bfloat16), ("lat", "dp")).astype(jnp.float32),
        lax.psum(bias_sum.astype(jnp.bfloat16), ("lat", "dp")).astype(jnp.float32),
    )
    normalizer = 1.0 / math.sqrt(
        micro * lax.axis_size("dp") * band_rows * lax.axis_size("lat") * longitude
    )
    kernel_grad = (kernel_total * normalizer).reshape(1, channels, 9, channels)
    bias_grad = (bias_total * normalizer)[None]
    return (last_outputs[None], adjoints[None], kernel_grad, bias_grad)


def solution(mesh):
    return jax.shard_map(
        per_device,
        mesh=mesh,
        in_specs=(
            P("dp", None, "lat", None),
            P("segment", None, None, None),
            P("segment", None),
            P(None, "dp", None, "lat", None),
        ),
        out_specs=(
            P("segment", "dp", None, "lat", None),
            P("segment", "dp", None, "lat", None),
            P("segment", None, None, None),
            P("segment", None),
        ),
        check_vma=False,
    )
```

profile of v0, /device:TPU:2, one launch (start us, length us, event | category | flops | bytes accessed | tf_op | source)
XLA Modules:
  0.0 2029.5 jit_solution(11901487231347078123)
XLA Ops:
  13.8 500.7 %while.48 = (s32[]{:T(128)}, bf16[192,2,128]{2,1,0:T(2,128)(2,1)}, bf16[4,192,2,128]{3,1,2,0:T(8,128)(2,1)S(1)}, bf16[8,192,2,128]{3,2,1,0:T(2,128)(2,1)}, bf16[...) while((s32[]{:T(128)}, bf16[192,2,128]{2,1,0:T(2,128)(2,1)}, ...), condition=%wide.region_3.4_spmd, body=%wide.region_0.3_spmd.sunk | while | flops 172425280 | bytes 14624630 | solution.py:134
  80.8 7.3 collective-permute-start.2
  95.0 11.4 collective-permute-done
  156.9 7.3 collective-permute-start.2
  181.2 7.3 collective-permute-start.2
  225.6 7.5 collective-permute-start.2
  245.9 7.0 collective-permute-start.2
  265.7 7.3 collective-permute-start.2
  306.4 7.4 collective-permute-start.2
  326.6 7.3 collective-permute-start.2
  340.8 15.1 collective-permute-done
  382.7 7.3 collective-permute-start.2
  434.2 7.3 collective-permute-start.2
  460.2 9.1 collective-permute-start.2
  482.4 7.6 collective-permute-start.2
  503.9 7.1 collective-permute-start.2
  517.5 1142.3 %while.49 = (s32[]{:T(128)}, bf16[192,2,128]{2,1,0:T(2,128)(2,1)}, bf16[4,192,2,128]{3,2,1,0:T(2,128)(2,1)}, f32[4,192,2,128]{3,2,1,0:T(2,128)}, f32[192,1728]{1...) while((s32[]{:T(128)}, bf16[192,2,128]{2,1,0:T(2,128)(2,1)}, ...), condition=%wide.region_8.9_spmd, body=%wide.region_4.8_spmd.sunk | while | flops 343953472 | bytes 20231204 | solution.py:193
  526.7 8.6 collective-permute-start.5
  573.4 9.4 collective-permute-start.5
  594.2 97.0 %collective-permute-done.3 = bf16[192,2,128]{2,1,0:T(2,128)(2,1)S(1)} collective-permute-done((bf16[192,2,128]{2,1,0:T(2,128)(2,1)}, bf16[192,2,128]{2,1,0:T(2,128)(2,1)S(1)}, u32[]{:S(2)}, u32[]{:S(2)}) %collective-permute-start.3) | collective-permute-done | bytes 98336 | tf_op jit(solution)/shard_map/while/body/eval_jaxpr/ppermute | solution.py:13
  694.5 7.0 collective-permute-start.5
  704.0 33.2 %conditional.5 = (f32[192,1728]{1,0:T(8,128)S(1)}, f32[192]{0:T(256)S(1)}, f32[192,2,128]{2,1,0:T(2,128)}, bf16[192,2,128]{2,1,0:T(2,128)(2,1)}) conditional(s32[]{:T(128)} %convert_element_type.170, (f32[192,1728]{1,0:T(8,128)S(1)}, f32[192]{0:T(256)S(1)}) %tuple.180, (s32[]{:T(128)}, s32[]{:T(128)}, pred[]{:T(512)}, pred[]{:T(512)}, ...), branch_computations={%region_5.5_spmd, %region_6.7_spmd.clone} | conditional | flops 343216128 | bytes 17083920 | solution.py:182
  749.2 11.7 collective-permute-start.5
  765.0 33.2 %conditional.5 = (f32[192,1728]{1,0:T(8,128)S(1)}, f32[192]{0:T(256)S(1)}, f32[192,2,128]{2,1,0:T(2,128)}, bf16[192,2,128]{2,1,0:T(2,128)(2,1)}) conditional(s32[]{:T(128)} %convert_element_type.170, (f32[192,1728]{1,0:T(8,128)S(1)}, f32[192]{0:T(256)S(1)}) %tuple.180, (s32[]{:T(128)}, s32[]{:T(128)}, pred[]{:T(512)}, pred[]{:T(512)}, ...), branch_computations={%region_5.5_spmd, %region_6.7_spmd.clone} | conditional | flops 343216128 | bytes 17083920 | solution.py:182
  821.1 33.2 %conditional.5 = (f32[192,1728]{1,0:T(8,128)S(1)}, f32[192]{0:T(256)S(1)}, f32[192,2,128]{2,1,0:T(2,128)}, bf16[192,2,128]{2,1,0:T(2,128)(2,1)}) conditional(s32[]{:T(128)} %convert_element_type.170, (f32[192,1728]{1,0:T(8,128)S(1)}, f32[192]{0:T(256)S(1)}) %tuple.180, (s32[]{:T(128)}, s32[]{:T(128)}, pred[]{:T(512)}, pred[]{:T(512)}, ...), branch_computations={%region_5.5_spmd, %region_6.7_spmd.clone} | conditional | flops 343216128 | bytes 17083920 | solution.py:182
  865.2 7.0 collective-permute-start.5
  874.7 33.2 %conditional.5 = (f32[192,1728]{1,0:T(8,128)S(1)}, f32[192]{0:T(256)S(1)}, f32[192,2,128]{2,1,0:T(2,128)}, bf16[192,2,128]{2,1,0:T(2,128)(2,1)}) conditional(s32[]{:T(128)} %convert_element_type.170, (f32[192,1728]{1,0:T(8,128)S(1)}, f32[192]{0:T(256)S(1)}) %tuple.180, (s32[]{:T(128)}, s32[]{:T(128)}, pred[]{:T(512)}, pred[]{:T(512)}, ...), branch_computations={%region_5.5_spmd, %region_6.7_spmd.clone} | conditional | flops 343216128 | bytes 17083920 | solution.py:182
  919.8 8.4 collective-permute-start.5
  934.9 33.9 %collective-permute-start.3 = (bf16[192,2,128]{2,1,0:T(2,128)(2,1)}, bf16[192,2,128]{2,1,0:T(2,128)(2,1)S(1)}, u32[]{:S(2)}, u32[]{:S(2)}) collective-permute-start(bf16[192,2,128]{2,1,0:T(2,128)(2,1)} %get-tuple-element.1480), channel_id=1, source_target_pairs={{0,224},{32,0},{64,32},{96,64},{128,96},{160,128},{192,160},{224,1... | collective-permute-start | bytes 294920 | tf_op jit(solution)/shard_map/while/body/eval_jaxpr/ppermute | solution.py:13
  974.5 9.2 collective-permute-start.5
  1001.2 7.0 collective-permute-start.5
  1014.9 30.2 %collective-permute-start.3 = (bf16[192,2,128]{2,1,0:T(2,128)(2,1)}, bf16[192,2,128]{2,1,0:T(2,128)(2,1)S(1)}, u32[]{:S(2)}, u32[]{:S(2)}) collective-permute-start(bf16[192,2,128]{2,1,0:T(2,128)(2,1)} %get-tuple-element.1480), channel_id=1, source_target_pairs={{0,224},{32,0},{64,32},{96,64},{128,96},{160,128},{192,160},{224,1... | collective-permute-start | bytes 294920 | tf_op jit(solution)/shard_map/while/body/eval_jaxpr/ppermute | solution.py:13
  1087.3 29.7 %collective-permute-start.3 = (bf16[192,2,128]{2,1,0:T(2,128)(2,1)}, bf16[192,2,128]{2,1,0:T(2,128)(2,1)S(1)}, u32[]{:S(2)}, u32[]{:S(2)}) collective-permute-start(bf16[192,2,128]{2,1,0:T(2,128)(2,1)} %get-tuple-element.1480), channel_id=1, source_target_pairs={{0,224},{32,0},{64,32},{96,64},{128,96},{160,128},{192,160},{224,1... | collective-permute-start | bytes 294920 | tf_op jit(solution)/shard_map/while/body/eval_jaxpr/ppermute | solution.py:13
  1145.6 13.3 collective-permute-start.5
  1164.7 30.2 %collective-permute-start.3 = (bf16[192,2,128]{2,1,0:T(2,128)(2,1)}, bf16[192,2,128]{2,1,0:T(2,128)(2,1)S(1)}, u32[]{:S(2)}, u32[]{:S(2)}) collective-permute-start(bf16[192,2,128]{2,1,0:T(2,128)(2,1)} %get-tuple-element.1480), channel_id=1, source_target_pairs={{0,224},{32,0},{64,32},{96,64},{128,96},{160,128},{192,160},{224,1... | collective-permute-start | bytes 294920 | tf_op jit(solution)/shard_map/while/body/eval_jaxpr/ppermute | solution.py:13
  1195.8 94.5 %collective-permute-done.3 = bf16[192,2,128]{2,1,0:T(2,128)(2,1)S(1)} collective-permute-done((bf16[192,2,128]{2,1,0:T(2,128)(2,1)}, bf16[192,2,128]{2,1,0:T(2,128)(2,1)S(1)}, u32[]{:S(2)}, u32[]{:S(2)}) %collective-permute-start.3) | collective-permute-done | bytes 98336 | tf_op jit(solution)/shard_map/while/body/eval_jaxpr/ppermute | solution.py:13
  1293.6 9.2 collective-permute-start.5
  1305.7 33.2 %conditional.5 = (f32[192,1728]{1,0:T(8,128)S(1)}, f32[192]{0:T(256)S(1)}, f32[192,2,128]{2,1,0:T(2,128)}, bf16[192,2,128]{2,1,0:T(2,128)(2,1)}) conditional(s32[]{:T(128)} %convert_element_type.170, (f32[192,1728]{1,0:T(8,128)S(1)}, f32[192]{0:T(256)S(1)}) %tuple.180, (s32[]{:T(128)}, s32[]{:T(128)}, pred[]{:T(512)}, pred[]{:T(512)}, ...), branch_computations={%region_5.5_spmd, %region_6.7_spmd.clone} | conditional | flops 343216128 | bytes 17083920 | solution.py:182
  1360.4 33.2 %conditional.5 = (f32[192,1728]{1,0:T(8,128)S(1)}, f32[192]{0:T(256)S(1)}, f32[192,2,128]{2,1,0:T(2,128)}, bf16[192,2,128]{2,1,0:T(2,128)(2,1)}) conditional(s32[]{:T(128)} %convert_element_type.170, (f32[192,1728]{1,0:T(8,128)S(1)}, f32[192]{0:T(256)S(1)}) %tuple.180, (s32[]{:T(128)}, s32[]{:T(128)}, pred[]{:T(512)}, pred[]{:T(512)}, ...), branch_computations={%region_5.5_spmd, %region_6.7_spmd.clone} | conditional | flops 343216128 | bytes 17083920 | solution.py:182
  1405.6 9.1 collective-permute-start.5
  1417.6 33.2 %conditional.5 = (f32[192,1728]{1,0:T(8,128)S(1)}, f32[192]{0:T(256)S(1)}, f32[192,2,128]{2,1,0:T(2,128)}, bf16[192,2,128]{2,1,0:T(2,128)(2,1)}) conditional(s32[]{:T(128)} %convert_element_type.170, (f32[192,1728]{1,0:T(8,128)S(1)}, f32[192]{0:T(256)S(1)}) %tuple.180, (s32[]{:T(128)}, s32[]{:T(128)}, pred[]{:T(512)}, pred[]{:T(512)}, ...), branch_computations={%region_5.5_spmd, %region_6.7_spmd.clone} | conditional | flops 343216128 | bytes 17083920 | solution.py:182
  1472.3 33.2 %conditional.5 = (f32[192,1728]{1,0:T(8,128)S(1)}, f32[192]{0:T(256)S(1)}, f32[192,2,128]{2,1,0:T(2,128)}, bf16[192,2,128]{2,1,0:T(2,128)(2,1)}) conditional(s32[]{:T(128)} %convert_element_type.170, (f32[192,1728]{1,0:T(8,128)S(1)}, f32[192]{0:T(256)S(1)}) %tuple.180, (s32[]{:T(128)}, s32[]{:T(128)}, pred[]{:T(512)}, pred[]{:T(512)}, ...), branch_computations={%region_5.5_spmd, %region_6.7_spmd.clone} | conditional | flops 343216128 | bytes 17083920 | solution.py:182
  1515.4 9.7 collective-permute-start.5
  1530.8 37.3 %collective-permute-start.3 = (bf16[192,2,128]{2,1,0:T(2,128)(2,1)}, bf16[192,2,128]{2,1,0:T(2,128)(2,1)S(1)}, u32[]{:S(2)}, u32[]{:S(2)}) collective-permute-start(bf16[192,2,128]{2,1,0:T(2,128)(2,1)} %get-tuple-element.1480), channel_id=1, source_target_pairs={{0,224},{32,0},{64,32},{96,64},{128,96},{160,128},{192,160},{224,1... | collective-permute-start | bytes 294920 | tf_op jit(solution)/shard_map/while/body/eval_jaxpr/ppermute | solution.py:13
  1597.3 8.3 collective-permute-start.5
  1612.2 29.8 %collective-permute-start.3 = (bf16[192,2,128]{2,1,0:T(2,128)(2,1)}, bf16[192,2,128]{2,1,0:T(2,128)(2,1)S(1)}, u32[]{:S(2)}, u32[]{:S(2)}) collective-permute-start(bf16[192,2,128]{2,1,0:T(2,128)(2,1)} %get-tuple-element.1480), channel_id=1, source_target_pairs={{0,224},{32,0},{64,32},{96,64},{128,96},{160,128},{192,160},{224,1... | collective-permute-start | bytes 294920 | tf_op jit(solution)/shard_map/while/body/eval_jaxpr/ppermute | solution.py:13
  1660.8 94.2 %psum.15 = bf16[192]{0:T(256)(128)(2,1)S(1)} all-reduce(bf16[192]{0:T(256)(128)(2,1)S(1)} %convert_element_type.117), channel_id=1, replica_groups=mesh['segment'=8,'lat'=16,'dp'=2] {'lat','dp'}, use_global_device_ids=true, to_apply=%region_10.11 | all-reduce | flops 192 | bytes 768 | tf_op jit(solution)/shard_map/psum | solution.py:198
  1755.5 261.1 %all-reduce.2.cloned.1.call-done = bf16[192,1728]{1,0:T(8,128)(2,1)} async-done(((bf16[192,1728]{1,0:T(8,128)(2,1)}), bf16[192,1728]{1,0:T(8,128)(2,1)}) %all-reduce.2.cloned.1.call-update) | async-done | bytes 663568 | tf_op jit(solution)/shard_map/psum | solution.py:197
  (1358 shorter events, 1098.2 us)
Async XLA Ops:
  7.2 2009.5 %all-reduce.2.cloned.1.call-start = ((), (), s32[]{:S(2)}) async-start(), calls=%async_computation | async-start | bytes 1376256 | tf_op jit(solution)/shard_map/psum | solution.py:197
  92.5 13.8 collective-permute-start
  224.3 9.6 collective-permute-start.1
  305.1 9.5 collective-permute-start.1
  338.4 17.6 collective-permute-start
  458.9 11.2 collective-permute-start.1
  460.2 11.2 collective-permute-start.2
  481.1 9.6 collective-permute-start.1
  482.4 10.4 collective-permute-start.2
  525.4 11.5 collective-permute-start.4
  526.7 12.5 collective-permute-start.5
  549.5 9.8 collective-permute-start.4
  572.1 12.3 collective-permute-start.4
  573.4 12.0 collective-permute-start.5
  588.9 102.3 %collective-permute-start.3 = (bf16[192,2,128]{2,1,0:T(2,128)(2,1)}, bf16[192,2,128]{2,1,0:T(2,128)(2,1)S(1)}, u32[]{:S(2)}, u32[]{:S(2)}) collective-permute-start(bf16[192,2,128]{2,1,0:T(2,128)(2,1)} %get-tuple-element.1480), channel_id=1, source_target_pairs={{0,224},{32,0},{64,32},{96,64},{128,96},{160,128},{192,160},{224,1... | collective-permute-start | bytes 294920 | tf_op jit(solution)/shard_map/while/body/eval_jaxpr/ppermute | solution.py:13
  693.2 9.9 collective-permute-start.4
  747.9 14.6 collective-permute-start.4
  749.2 15.5 collective-permute-start.5
  808.7 9.5 collective-permute-start.4
  810.0 10.8 collective-permute-start.5
  863.9 9.9 collective-permute-start.4
  918.5 11.4 collective-permute-start.4
  919.8 11.6 collective-permute-start.5
  934.9 36.4 %collective-permute-start.3 = (bf16[192,2,128]{2,1,0:T(2,128)(2,1)}, bf16[192,2,128]{2,1,0:T(2,128)(2,1)S(1)}, u32[]{:S(2)}, u32[]{:S(2)}) collective-permute-start(bf16[192,2,128]{2,1,0:T(2,128)(2,1)} %get-tuple-element.1480), channel_id=1, source_target_pairs={{0,224},{32,0},{64,32},{96,64},{128,96},{160,128},{192,160},{224,1... | collective-permute-start | bytes 294920 | tf_op jit(solution)/shard_map/while/body/eval_jaxpr/ppermute | solution.py:13
  973.2 12.1 collective-permute-start.4
  974.5 11.4 collective-permute-start.5
  999.9 10.0 collective-permute-start.4
  1001.2 10.2 collective-permute-start.5
  1014.9 32.7 %collective-permute-start.3 = (bf16[192,2,128]{2,1,0:T(2,128)(2,1)}, bf16[192,2,128]{2,1,0:T(2,128)(2,1)S(1)}, u32[]{:S(2)}, u32[]{:S(2)}) collective-permute-start(bf16[192,2,128]{2,1,0:T(2,128)(2,1)} %get-tuple-element.1480), channel_id=1, source_target_pairs={{0,224},{32,0},{64,32},{96,64},{128,96},{160,128},{192,160},{224,1... | collective-permute-start | bytes 294920 | tf_op jit(solution)/shard_map/while/body/eval_jaxpr/ppermute | solution.py:13
  1050.9 9.6 collective-permute-start.5
  1074.3 9.5 collective-permute-start.5
  1087.3 32.2 %collective-permute-start.3 = (bf16[192,2,128]{2,1,0:T(2,128)(2,1)}, bf16[192,2,128]{2,1,0:T(2,128)(2,1)S(1)}, u32[]{:S(2)}, u32[]{:S(2)}) collective-permute-start(bf16[192,2,128]{2,1,0:T(2,128)(2,1)} %get-tuple-element.1480), channel_id=1, source_target_pairs={{0,224},{32,0},{64,32},{96,64},{128,96},{160,128},{192,160},{224,1... | collective-permute-start | bytes 294920 | tf_op jit(solution)/shard_map/while/body/eval_jaxpr/ppermute | solution.py:13
  1144.3 16.3 collective-permute-start.4
  1145.6 15.5 collective-permute-start.5
  1164.7 125.7 %collective-permute-start.3 = (bf16[192,2,128]{2,1,0:T(2,128)(2,1)}, bf16[192,2,128]{2,1,0:T(2,128)(2,1)S(1)}, u32[]{:S(2)}, u32[]{:S(2)}) collective-permute-start(bf16[192,2,128]{2,1,0:T(2,128)(2,1)} %get-tuple-element.1480), channel_id=1, source_target_pairs={{0,224},{32,0},{64,32},{96,64},{128,96},{160,128},{192,160},{224,1... | collective-permute-start | bytes 294920 | tf_op jit(solution)/shard_map/while/body/eval_jaxpr/ppermute | solution.py:13
  1292.3 12.1 collective-permute-start.4
  1293.6 11.7 collective-permute-start.5
  1349.6 9.9 collective-permute-start.4
  1404.3 12.0 collective-permute-start.4
  1405.6 11.6 collective-permute-start.5
  1461.5 9.9 collective-permute-start.4
  1514.1 12.6 collective-permute-start.4
  1515.4 11.8 collective-permute-start.5
  1530.8 39.8 %collective-permute-start.3 = (bf16[192,2,128]{2,1,0:T(2,128)(2,1)}, bf16[192,2,128]{2,1,0:T(2,128)(2,1)S(1)}, u32[]{:S(2)}, u32[]{:S(2)}) collective-permute-start(bf16[192,2,128]{2,1,0:T(2,128)(2,1)} %get-tuple-element.1480), channel_id=1, source_target_pairs={{0,224},{32,0},{64,32},{96,64},{128,96},{160,128},{192,160},{224,1... | collective-permute-start | bytes 294920 | tf_op jit(solution)/shard_map/while/body/eval_jaxpr/ppermute | solution.py:13
  1572.5 9.9 collective-permute-start.4
  1596.0 11.2 collective-permute-start.4
  1597.3 11.4 collective-permute-start.5
  1612.2 32.3 %collective-permute-start.3 = (bf16[192,2,128]{2,1,0:T(2,128)(2,1)}, bf16[192,2,128]{2,1,0:T(2,128)(2,1)S(1)}, u32[]{:S(2)}, u32[]{:S(2)}) collective-permute-start(bf16[192,2,128]{2,1,0:T(2,128)(2,1)} %get-tuple-element.1480), channel_id=1, source_target_pairs={{0,224},{32,0},{64,32},{96,64},{128,96},{160,128},{192,160},{224,1... | collective-permute-start | bytes 294920 | tf_op jit(solution)/shard_map/while/body/eval_jaxpr/ppermute | solution.py:13
  (111 other events, 931.8 us)
Sparse Core Ops, SparseCore 0:
  1660.9 355.7 all-reduce.1
where the time goes:
time: 2040 us; the launch traced here: 2030 us
  waiting for transfers between devices  671 us (33%)
  starting transfers between devices  631 us (31%)
  local copies, waits for them, and re-layouts  373 us (18%)
  other arithmetic  222 us (11%)
  blocking collectives  94.2 us (5%)
    ppermute x44, waiting for transfers between devices, passed_along(): return lax.ppermute(value, axis, pairs)  362 us
    ppermute x44, starting transfers between devices, padded_2(): lax.ppermute(lax.slice_in_dim(block, block.shape[dim] - width, None, axis...  334 us
    psum x1, waiting for transfers between devices, per_device(): lax.psum(kernel_sum.astype(jnp.bfloat16), ('lat', 'dp')).astype(jnp.float32)  261 us
    ppermute x44, starting transfers between devices, passed_along(): return lax.ppermute(value, axis, pairs)  240 us
    dynamic_slice x132, local copies, waits for them, and re-layouts, put_slot(): previous = lax.dynamic_index_in_dim(buffer, slot, 0, keepdims=False)  105 us
    psum x1, blocking collectives, per_device(): lax.psum(bias_sum.astype(jnp.bfloat16), ('lat', 'dp')).astype(jnp.float32)  94.2 us
    another operation x80, local copies, waits for them, and re-layouts, back_columns(): stacked = jnp.stack(pieces, axis=0)  68.2 us
    concatenate x48, other arithmetic, back_columns(): pieces.append(jnp.roll(strip, col_tap - 1, axis=2))  63.6 us
  transfers between devices with their start and end apart: 133, of which 89 were waited for; matrix products, arithmetic and copies ran while one was open for 6% of the time, Pallas kernels for 0%

commit v1 on v0

--- a/solution.py
+++ b/solution.py
@@ -194,7 +194,7 @@
         0, tick_count, backward_tick, backward_start
     )
     kernel_total, bias_total = (
-        lax.psum(kernel_sum.astype(jnp.bfloat16), ("lat", "dp")).astype(jnp.float32),
+        lax.psum(lax.psum(kernel_sum.astype(jnp.bfloat16), "dp"), "lat").astype(jnp.float32),
         lax.psum(bias_sum.astype(jnp.bfloat16), ("lat", "dp")).astype(jnp.float32),
     )
     normalizer = 1.0 / math.sqrt(

time: 2040 us -> 1970 us (0.966)
  waiting for transfers between devices: 671 us -> 621 us
  blocking collectives: 94.2 us -> 70.6 us
    psum x1 -> x2, waiting for transfers between devices: 261 us -> 211 us  [the longest x1 119 us: per_device(): lax.psum(kernel_sum.astype(jnp.bfloat16), 'dp')]
    psum x1, blocking collectives: 94.2 us -> 70.6 us  [per_device(): lax.psum(bias_sum.astype(jnp.bfloat16), ('lat', 'dp')).astype(jnp.float32)]
  transfers between devices with their start and end apart: 133 -> 134, of which waited for: 89 -> 90; matrix products, arithmetic and copies ran while one was open for 6% -> 6% of each run, Pallas kernels for 0% -> 0%
where the time goes in v1:
time: 1970 us; the launch traced here: 1950 us
  starting transfers between devices  632 us (32%)
  waiting for transfers between devices  621 us (32%)
  local copies, waits for them, and re-layouts  357 us (18%)
  other arithmetic  236 us (12%)
  blocking collectives  70.6 us (4%)
    ppermute x44, waiting for transfers between devices, passed_along(): return lax.ppermute(value, axis, pairs)  363 us
    ppermute x44, starting transfers between devices, padded_2(): lax.ppermute(lax.slice_in_dim(block, block.shape[dim] - width, None, axis...  335 us
    ppermute x44, starting transfers between devices, passed_along(): return lax.ppermute(value, axis, pairs)  240 us
    psum x1, waiting for transfers between devices, per_device(): lax.psum(kernel_sum.astype(jnp.bfloat16), 'dp')  119 us
    dynamic_slice x132, local copies, waits for them, and re-layouts, put_slot(): previous = lax.dynamic_index_in_dim(buffer, slot, 0, keepdims=False)  104 us
    psum x1, waiting for transfers between devices, per_device(): lax.psum(lax.psum(kernel_sum.astype(jnp.bfloat16), 'dp'), 'lat')  92.1 us
    dynamic_update_slice x88, other arithmetic, put_slot(): lax.dynamic_update_index_in_dim(buffer, jnp.where(flag, value, previous),...  75.2 us
    psum x1, blocking collectives, per_device(): lax.psum(bias_sum.astype(jnp.bfloat16), ('lat', 'dp')).astype(jnp.float32)  70.6 us
  transfers between devices with their start and end apart: 134, of which 90 were waited for; matrix products, arithmetic and copies ran while one was open for 6% of the time, Pallas kernels for 0%

profile of v1, /device:TPU:2, one launch (start us, length us, event | category | flops | bytes accessed | tf_op | source)
XLA Modules:
  0.0 1954.8 jit_solution(3103073369984927063)
XLA Ops:
  13.4 499.9 %while.48 = (s32[]{:T(128)}, bf16[192,2,128]{2,1,0:T(2,128)(2,1)}, bf16[4,192,2,128]{3,1,2,0:T(8,128)(2,1)S(1)}, bf16[8,192,2,128]{3,2,1,0:T(2,128)(2,1)}, bf16[...) while((s32[]{:T(128)}, bf16[192,2,128]{2,1,0:T(2,128)(2,1)}, ...), condition=%wide.region_3.4_spmd, body=%wide.region_0.3_spmd.sunk | while | flops 172425280 | bytes 14624630 | solution.py:134
  80.2 7.3 collective-permute-start.2
  94.3 11.4 collective-permute-done
  156.2 7.3 collective-permute-start.2
  180.5 7.3 collective-permute-start.2
  205.0 7.1 collective-permute-start.2
  224.9 7.8 collective-permute-start.2
  265.1 7.3 collective-permute-start.2
  286.0 7.0 collective-permute-start.2
  305.8 7.3 collective-permute-start.2
  325.8 7.3 collective-permute-start.2
  340.3 14.6 collective-permute-done
  381.6 7.3 collective-permute-start.2
  433.1 7.4 collective-permute-start.2
  459.1 9.1 collective-permute-start.2
  481.2 7.6 collective-permute-start.2
  502.8 7.1 collective-permute-start.2
  516.3 1142.4 %while.49 = (s32[]{:T(128)}, bf16[192,2,128]{2,1,0:T(2,128)(2,1)}, bf16[4,192,2,128]{3,2,1,0:T(2,128)(2,1)}, f32[4,192,2,128]{3,2,1,0:T(2,128)}, f32[192,1728]{1...) while((s32[]{:T(128)}, bf16[192,2,128]{2,1,0:T(2,128)(2,1)}, ...), condition=%wide.region_8.9_spmd, body=%wide.region_4.8_spmd.sunk | while | flops 343953472 | bytes 20231204 | solution.py:193
  525.5 8.5 collective-permute-start.5
  549.2 7.9 collective-permute-start.5
  574.0 7.6 collective-permute-start.5
  592.5 97.7 %collective-permute-done.3 = bf16[192,2,128]{2,1,0:T(2,128)(2,1)S(1)} collective-permute-done((bf16[192,2,128]{2,1,0:T(2,128)(2,1)}, bf16[192,2,128]{2,1,0:T(2,128)(2,1)S(1)}, u32[]{:S(2)}, u32[]{:S(2)}) %collective-permute-start.3) | collective-permute-done | bytes 98336 | tf_op jit(solution)/shard_map/while/body/eval_jaxpr/ppermute | solution.py:13
  702.9 33.2 %conditional.5 = (f32[192,1728]{1,0:T(8,128)S(1)}, f32[192]{0:T(256)S(1)}, f32[192,2,128]{2,1,0:T(2,128)}, bf16[192,2,128]{2,1,0:T(2,128)(2,1)}) conditional(s32[]{:T(128)} %convert_element_type.170, (f32[192,1728]{1,0:T(8,128)S(1)}, f32[192]{0:T(256)S(1)}) %tuple.180, (s32[]{:T(128)}, s32[]{:T(128)}, pred[]{:T(512)}, pred[]{:T(512)}, ...), branch_computations={%region_5.5_spmd, %region_6.7_spmd.clone} | conditional | flops 343216128 | bytes 17083920 | solution.py:182
  748.0 11.8 collective-permute-start.5
  763.9 33.2 %conditional.5 = (f32[192,1728]{1,0:T(8,128)S(1)}, f32[192]{0:T(256)S(1)}, f32[192,2,128]{2,1,0:T(2,128)}, bf16[192,2,128]{2,1,0:T(2,128)(2,1)}) conditional(s32[]{:T(128)} %convert_element_type.170, (f32[192,1728]{1,0:T(8,128)S(1)}, f32[192]{0:T(256)S(1)}) %tuple.180, (s32[]{:T(128)}, s32[]{:T(128)}, pred[]{:T(512)}, pred[]{:T(512)}, ...), branch_computations={%region_5.5_spmd, %region_6.7_spmd.clone} | conditional | flops 343216128 | bytes 17083920 | solution.py:182
  820.2 33.2 %conditional.5 = (f32[192,1728]{1,0:T(8,128)S(1)}, f32[192]{0:T(256)S(1)}, f32[192,2,128]{2,1,0:T(2,128)}, bf16[192,2,128]{2,1,0:T(2,128)(2,1)}) conditional(s32[]{:T(128)} %convert_element_type.170, (f32[192,1728]{1,0:T(8,128)S(1)}, f32[192]{0:T(256)S(1)}) %tuple.180, (s32[]{:T(128)}, s32[]{:T(128)}, pred[]{:T(512)}, pred[]{:T(512)}, ...), branch_computations={%region_5.5_spmd, %region_6.7_spmd.clone} | conditional | flops 343216128 | bytes 17083920 | solution.py:182
  873.7 33.2 %conditional.5 = (f32[192,1728]{1,0:T(8,128)S(1)}, f32[192]{0:T(256)S(1)}, f32[192,2,128]{2,1,0:T(2,128)}, bf16[192,2,128]{2,1,0:T(2,128)(2,1)}) conditional(s32[]{:T(128)} %convert_element_type.170, (f32[192,1728]{1,0:T(8,128)S(1)}, f32[192]{0:T(256)S(1)}) %tuple.180, (s32[]{:T(128)}, s32[]{:T(128)}, pred[]{:T(512)}, pred[]{:T(512)}, ...), branch_computations={%region_5.5_spmd, %region_6.7_spmd.clone} | conditional | flops 343216128 | bytes 17083920 | solution.py:182
  918.8 8.4 collective-permute-start.5
  933.9 33.9 %collective-permute-start.3 = (bf16[192,2,128]{2,1,0:T(2,128)(2,1)}, bf16[192,2,128]{2,1,0:T(2,128)(2,1)S(1)}, u32[]{:S(2)}, u32[]{:S(2)}) collective-permute-start(bf16[192,2,128]{2,1,0:T(2,128)(2,1)} %get-tuple-element.1480), channel_id=1, source_target_pairs={{0,224},{32,0},{64,32},{96,64},{128,96},{160,128},{192,160},{224,1... | collective-permute-start | bytes 294920 | tf_op jit(solution)/shard_map/while/body/eval_jaxpr/ppermute | solution.py:13
  973.5 9.2 collective-permute-start.5
  1013.8 30.2 %collective-permute-start.3 = (bf16[192,2,128]{2,1,0:T(2,128)(2,1)}, bf16[192,2,128]{2,1,0:T(2,128)(2,1)S(1)}, u32[]{:S(2)}, u32[]{:S(2)}) collective-permute-start(bf16[192,2,128]{2,1,0:T(2,128)(2,1)} %get-tuple-element.1480), channel_id=1, source_target_pairs={{0,224},{32,0},{64,32},{96,64},{128,96},{160,128},{192,160},{224,1... | collective-permute-start | bytes 294920 | tf_op jit(solution)/shard_map/while/body/eval_jaxpr/ppermute | solution.py:13
  1086.3 29.7 %collective-permute-start.3 = (bf16[192,2,128]{2,1,0:T(2,128)(2,1)}, bf16[192,2,128]{2,1,0:T(2,128)(2,1)S(1)}, u32[]{:S(2)}, u32[]{:S(2)}) collective-permute-start(bf16[192,2,128]{2,1,0:T(2,128)(2,1)} %get-tuple-element.1480), channel_id=1, source_target_pairs={{0,224},{32,0},{64,32},{96,64},{128,96},{160,128},{192,160},{224,1... | collective-permute-start | bytes 294920 | tf_op jit(solution)/shard_map/while/body/eval_jaxpr/ppermute | solution.py:13
  1144.6 13.3 collective-permute-start.5
  1163.6 30.2 %collective-permute-start.3 = (bf16[192,2,128]{2,1,0:T(2,128)(2,1)}, bf16[192,2,128]{2,1,0:T(2,128)(2,1)S(1)}, u32[]{:S(2)}, u32[]{:S(2)}) collective-permute-start(bf16[192,2,128]{2,1,0:T(2,128)(2,1)} %get-tuple-element.1480), channel_id=1, source_target_pairs={{0,224},{32,0},{64,32},{96,64},{128,96},{160,128},{192,160},{224,1... | collective-permute-start | bytes 294920 | tf_op jit(solution)/shard_map/while/body/eval_jaxpr/ppermute | solution.py:13
  1194.7 94.5 %collective-permute-done.3 = bf16[192,2,128]{2,1,0:T(2,128)(2,1)S(1)} collective-permute-done((bf16[192,2,128]{2,1,0:T(2,128)(2,1)}, bf16[192,2,128]{2,1,0:T(2,128)(2,1)S(1)}, u32[]{:S(2)}, u32[]{:S(2)}) %collective-permute-start.3) | collective-permute-done | bytes 98336 | tf_op jit(solution)/shard_map/while/body/eval_jaxpr/ppermute | solution.py:13
  1292.5 9.2 collective-permute-start.5
  1304.5 33.2 %conditional.5 = (f32[192,1728]{1,0:T(8,128)S(1)}, f32[192]{0:T(256)S(1)}, f32[192,2,128]{2,1,0:T(2,128)}, bf16[192,2,128]{2,1,0:T(2,128)(2,1)}) conditional(s32[]{:T(128)} %convert_element_type.170, (f32[192,1728]{1,0:T(8,128)S(1)}, f32[192]{0:T(256)S(1)}) %tuple.180, (s32[]{:T(128)}, s32[]{:T(128)}, pred[]{:T(512)}, pred[]{:T(512)}, ...), branch_computations={%region_5.5_spmd, %region_6.7_spmd.clone} | conditional | flops 343216128 | bytes 17083920 | solution.py:182
  1359.3 33.2 %conditional.5 = (f32[192,1728]{1,0:T(8,128)S(1)}, f32[192]{0:T(256)S(1)}, f32[192,2,128]{2,1,0:T(2,128)}, bf16[192,2,128]{2,1,0:T(2,128)(2,1)}) conditional(s32[]{:T(128)} %convert_element_type.170, (f32[192,1728]{1,0:T(8,128)S(1)}, f32[192]{0:T(256)S(1)}) %tuple.180, (s32[]{:T(128)}, s32[]{:T(128)}, pred[]{:T(512)}, pred[]{:T(512)}, ...), branch_computations={%region_5.5_spmd, %region_6.7_spmd.clone} | conditional | flops 343216128 | bytes 17083920 | solution.py:182
  1404.5 9.1 collective-permute-start.5
  1416.5 33.2 %conditional.5 = (f32[192,1728]{1,0:T(8,128)S(1)}, f32[192]{0:T(256)S(1)}, f32[192,2,128]{2,1,0:T(2,128)}, bf16[192,2,128]{2,1,0:T(2,128)(2,1)}) conditional(s32[]{:T(128)} %convert_element_type.170, (f32[192,1728]{1,0:T(8,128)S(1)}, f32[192]{0:T(256)S(1)}) %tuple.180, (s32[]{:T(128)}, s32[]{:T(128)}, pred[]{:T(512)}, pred[]{:T(512)}, ...), branch_computations={%region_5.5_spmd, %region_6.7_spmd.clone} | conditional | flops 343216128 | bytes 17083920 | solution.py:182
  1471.2 33.2 %conditional.5 = (f32[192,1728]{1,0:T(8,128)S(1)}, f32[192]{0:T(256)S(1)}, f32[192,2,128]{2,1,0:T(2,128)}, bf16[192,2,128]{2,1,0:T(2,128)(2,1)}) conditional(s32[]{:T(128)} %convert_element_type.170, (f32[192,1728]{1,0:T(8,128)S(1)}, f32[192]{0:T(256)S(1)}) %tuple.180, (s32[]{:T(128)}, s32[]{:T(128)}, pred[]{:T(512)}, pred[]{:T(512)}, ...), branch_computations={%region_5.5_spmd, %region_6.7_spmd.clone} | conditional | flops 343216128 | bytes 17083920 | solution.py:182
  1514.3 9.7 collective-permute-start.5
  1529.7 37.3 %collective-permute-start.3 = (bf16[192,2,128]{2,1,0:T(2,128)(2,1)}, bf16[192,2,128]{2,1,0:T(2,128)(2,1)S(1)}, u32[]{:S(2)}, u32[]{:S(2)}) collective-permute-start(bf16[192,2,128]{2,1,0:T(2,128)(2,1)} %get-tuple-element.1480), channel_id=1, source_target_pairs={{0,224},{32,0},{64,32},{96,64},{128,96},{160,128},{192,160},{224,1... | collective-permute-start | bytes 294920 | tf_op jit(solution)/shard_map/while/body/eval_jaxpr/ppermute | solution.py:13
  1596.2 8.3 collective-permute-start.5
  1611.1 29.8 %collective-permute-start.3 = (bf16[192,2,128]{2,1,0:T(2,128)(2,1)}, bf16[192,2,128]{2,1,0:T(2,128)(2,1)S(1)}, u32[]{:S(2)}, u32[]{:S(2)}) collective-permute-start(bf16[192,2,128]{2,1,0:T(2,128)(2,1)} %get-tuple-element.1480), channel_id=1, source_target_pairs={{0,224},{32,0},{64,32},{96,64},{128,96},{160,128},{192,160},{224,1... | collective-permute-start | bytes 294920 | tf_op jit(solution)/shard_map/while/body/eval_jaxpr/ppermute | solution.py:13
  1659.7 119.0 %all-reduce.3.cloned.1.call-done = bf16[192,1728]{1,0:T(8,128)(2,1)} async-done(((bf16[192,1728]{1,0:T(8,128)(2,1)}), bf16[192,1728]{1,0:T(8,128)(2,1)}) %all-reduce.3.cloned.1.call-update) | async-done | bytes 663568 | tf_op jit(solution)/shard_map/psum | solution.py:197
  1778.7 70.6 %psum.23 = bf16[192]{0:T(256)(128)(2,1)S(1)} all-reduce(bf16[192]{0:T(256)(128)(2,1)S(1)} %convert_element_type.117), channel_id=1, replica_groups=mesh['segment'=8,'lat'=16,'dp'=2] {'lat','dp'}, use_global_device_ids=true, to_apply=%region_11.12 | all-reduce | flops 192 | bytes 768 | tf_op jit(solution)/shard_map/psum | solution.py:198
  1849.9 92.1 %all-reduce.5.cloned.1.call-done = bf16[192,1728]{1,0:T(8,128)(2,1)} async-done(((bf16[192,1728]{1,0:T(8,128)(2,1)}), bf16[192,1728]{1,0:T(8,128)(2,1)}) %all-reduce.5.cloned.1.call-update) | async-done | bytes 663568 | tf_op jit(solution)/shard_map/psum | solution.py:197
  (1361 shorter events, 1104.6 us)
Async XLA Ops:
  7.2 1771.5 %all-reduce.3.cloned.1.call-start = ((), (), s32[]{:S(2)}) async-start(), calls=%async_computation | async-start | bytes 1376256 | tf_op jit(solution)/shard_map/psum | solution.py:197
  91.9 13.8 collective-permute-start
  223.6 9.8 collective-permute-start.1
  337.9 17.0 collective-permute-start
  457.8 11.2 collective-permute-start.1
  459.1 11.1 collective-permute-start.2
  479.9 9.6 collective-permute-start.1
  481.2 10.6 collective-permute-start.2
  524.2 11.5 collective-permute-start.4
  525.5 10.7 collective-permute-start.5
  547.9 10.8 collective-permute-start.4
  549.2 11.1 collective-permute-start.5
  572.7 10.6 collective-permute-start.4
  574.0 10.3 collective-permute-start.5
  587.8 102.3 %collective-permute-start.3 = (bf16[192,2,128]{2,1,0:T(2,128)(2,1)}, bf16[192,2,128]{2,1,0:T(2,128)(2,1)S(1)}, u32[]{:S(2)}, u32[]{:S(2)}) collective-permute-start(bf16[192,2,128]{2,1,0:T(2,128)(2,1)} %get-tuple-element.1480), channel_id=1, source_target_pairs={{0,224},{32,0},{64,32},{96,64},{128,96},{160,128},{192,160},{224,1... | collective-permute-start | bytes 294920 | tf_op jit(solution)/shard_map/while/body/eval_jaxpr/ppermute | solution.py:13
  692.1 9.9 collective-permute-start.4
  746.7 14.8 collective-permute-start.4
  748.0 15.5 collective-permute-start.5
  807.6 9.9 collective-permute-start.4
  808.9 10.9 collective-permute-start.5
  862.9 9.9 collective-permute-start.4
  917.5 11.4 collective-permute-start.4
  918.8 11.6 collective-permute-start.5
  933.9 36.4 %collective-permute-start.3 = (bf16[192,2,128]{2,1,0:T(2,128)(2,1)}, bf16[192,2,128]{2,1,0:T(2,128)(2,1)S(1)}, u32[]{:S(2)}, u32[]{:S(2)}) collective-permute-start(bf16[192,2,128]{2,1,0:T(2,128)(2,1)} %get-tuple-element.1480), channel_id=1, source_target_pairs={{0,224},{32,0},{64,32},{96,64},{128,96},{160,128},{192,160},{224,1... | collective-permute-start | bytes 294920 | tf_op jit(solution)/shard_map/while/body/eval_jaxpr/ppermute | solution.py:13
  972.2 12.1 collective-permute-start.4
  973.5 11.4 collective-permute-start.5
  998.9 9.8 collective-permute-start.4
  1000.2 10.1 collective-permute-start.5
  1013.8 32.7 %collective-permute-start.3 = (bf16[192,2,128]{2,1,0:T(2,128)(2,1)}, bf16[192,2,128]{2,1,0:T(2,128)(2,1)S(1)}, u32[]{:S(2)}, u32[]{:S(2)}) collective-permute-start(bf16[192,2,128]{2,1,0:T(2,128)(2,1)} %get-tuple-element.1480), channel_id=1, source_target_pairs={{0,224},{32,0},{64,32},{96,64},{128,96},{160,128},{192,160},{224,1... | collective-permute-start | bytes 294920 | tf_op jit(solution)/shard_map/while/body/eval_jaxpr/ppermute | solution.py:13
  1049.8 9.6 collective-permute-start.5
  1086.3 32.2 %collective-permute-start.3 = (bf16[192,2,128]{2,1,0:T(2,128)(2,1)}, bf16[192,2,128]{2,1,0:T(2,128)(2,1)S(1)}, u32[]{:S(2)}, u32[]{:S(2)}) collective-permute-start(bf16[192,2,128]{2,1,0:T(2,128)(2,1)} %get-tuple-element.1480), channel_id=1, source_target_pairs={{0,224},{32,0},{64,32},{96,64},{128,96},{160,128},{192,160},{224,1... | collective-permute-start | bytes 294920 | tf_op jit(solution)/shard_map/while/body/eval_jaxpr/ppermute | solution.py:13
  1143.3 16.2 collective-permute-start.4
  1144.6 15.5 collective-permute-start.5
  1163.6 125.7 %collective-permute-start.3 = (bf16[192,2,128]{2,1,0:T(2,128)(2,1)}, bf16[192,2,128]{2,1,0:T(2,128)(2,1)S(1)}, u32[]{:S(2)}, u32[]{:S(2)}) collective-permute-start(bf16[192,2,128]{2,1,0:T(2,128)(2,1)} %get-tuple-element.1480), channel_id=1, source_target_pairs={{0,224},{32,0},{64,32},{96,64},{128,96},{160,128},{192,160},{224,1... | collective-permute-start | bytes 294920 | tf_op jit(solution)/shard_map/while/body/eval_jaxpr/ppermute | solution.py:13
  1291.2 12.1 collective-permute-start.4
  1292.5 11.7 collective-permute-start.5
  1348.5 9.9 collective-permute-start.4
  1403.2 12.0 collective-permute-start.4
  1404.5 11.6 collective-permute-start.5
  1460.4 9.9 collective-permute-start.4
  1513.0 12.6 collective-permute-start.4
  1514.3 11.9 collective-permute-start.5
  1529.7 39.8 %collective-permute-start.3 = (bf16[192,2,128]{2,1,0:T(2,128)(2,1)}, bf16[192,2,128]{2,1,0:T(2,128)(2,1)S(1)}, u32[]{:S(2)}, u32[]{:S(2)}) collective-permute-start(bf16[192,2,128]{2,1,0:T(2,128)(2,1)} %get-tuple-element.1480), channel_id=1, source_target_pairs={{0,224},{32,0},{64,32},{96,64},{128,96},{160,128},{192,160},{224,1... | collective-permute-start | bytes 294920 | tf_op jit(solution)/shard_map/while/body/eval_jaxpr/ppermute | solution.py:13
  1571.4 9.9 collective-permute-start.4
  1594.9 11.2 collective-permute-start.4
  1596.2 11.4 collective-permute-start.5
  1611.1 32.3 %collective-permute-start.3 = (bf16[192,2,128]{2,1,0:T(2,128)(2,1)}, bf16[192,2,128]{2,1,0:T(2,128)(2,1)S(1)}, u32[]{:S(2)}, u32[]{:S(2)}) collective-permute-start(bf16[192,2,128]{2,1,0:T(2,128)(2,1)} %get-tuple-element.1480), channel_id=1, source_target_pairs={{0,224},{32,0},{64,32},{96,64},{128,96},{160,128},{192,160},{224,1... | collective-permute-start | bytes 294920 | tf_op jit(solution)/shard_map/while/body/eval_jaxpr/ppermute | solution.py:13
  1659.7 282.3 %all-reduce.5.cloned.1.call-start = ((), (), s32[]{:S(2)}) async-start(), calls=%async_computation.1 | async-start | bytes 1376256 | tf_op jit(solution)/shard_map/psum | solution.py:197
  (112 other events, 943.0 us)
Sparse Core Ops, SparseCore 0:
  1659.8 118.8 all-reduce.2
  1781.3 160.6 all-reduce.4
